TPU v7x, 256 devices: a whole 4x4x8 slice. The times are simulated.
256 devices in a mesh: aux: 16 (over x, z_hi), pair: 16 (over y, z_lo, core).
Axes of the slice: x: 4, y: 4, z: 8 (z_hi: 4, z_lo: 2; z = z_hi * 2 + z_lo), core: 2. Of those that a mesh axis runs over, the one named last changes fastest.
Arguments:
- amplitudes: bfloat16 [512, 36864], P(('aux', 'pair')), may hold values from -6 to 6
- factors: bfloat16 [256, 36864], P('aux'), may hold values from -0.109375 to 0.109375
- sources: int32 [512, 8], P(('aux', 'pair')), may hold values from 0 to 511, as said below
- weights: float32 [512, 8], P(('aux', 'pair')), may hold values from -0.5 to 0.5
- flip_flags: int32 [512, 8], P(('aux', 'pair')), may hold values 0 or 1
Outputs:
- residual: float32 [512, 36864], P(('aux', 'pair'))
Inputs may be any that keep to these rules, and one draw needn't show every extreme that they name: `sources`: every source lies in the same aligned block of 32 pairs as its target pair.
All inputs are finite; a program needn't handle non-finite values. No bound on the sum of `flip_flags` on one device may be relied on, other than what follows from the above.
Results may differ from a plain program's by a relative error of at most 0.0026.
Values may be sent and summed in bfloat16 or wider, within the bound.
No kernel may reach another device: no remote copies, remote signals or barrier semaphores. Data moves between devices by JAX's collectives and lax.ppermute only.
A program may use at most 128 MiB of HBM per device.

v0:
```python
import jax
import jax.numpy as jnp
from jax import lax
from jax.sharding import PartitionSpec as P

V = 192


def ladder_terms(amp_flat, fac_flat):
    virtual = V
    pair_count = amp_flat.shape[0]
    aux_count = fac_flat.shape[0]
    amp_blocks = amp_flat.reshape(pair_count, virtual, virtual)
    fac_blocks = fac_flat.reshape(aux_count, virtual, virtual)
    pair_step = 2
    aux_step = 16
    stacked = fac_blocks.reshape(aux_count // aux_step, aux_step, virtual, virtual)
    grouped = amp_blocks.reshape(pair_count // pair_step, pair_step, virtual, virtual)

    def one_group(members):

        def advance(running, factor_set):
            halfway = jnp.einsum(
                "qab,pbc->pqac", factor_set, members, preferred_element_type=jnp.float32
            ).astype(jnp.bfloat16)
            return (
                running
                + jnp.einsum(
                    "pqac,qdc->pad", halfway, factor_set, preferred_element_type=jnp.float32
                ),
                None,
            )

        initial = jnp.zeros((pair_step, virtual, virtual), jnp.float32)
        result, unused = lax.scan(advance, initial, stacked)
        return result

    return lax.map(one_group, grouped).reshape(pair_count, virtual * virtual)


def local(amplitudes, factors, sources, weights, flip_flags):
    pair_count = amplitudes.shape[0]
    ladder = ladder_terms(amplitudes, lax.all_gather(factors, "aux", axis=0, tiled=True))
    neighbours = lax.all_gather(amplitudes, "pair", axis=0, tiled=True).astype(jnp.float32)
    group_size = neighbours.shape[0]
    local_index = sources % group_size
    onehot = (
        local_index[:, :, None] == jnp.arange(group_size, dtype=jnp.int32)[None, None, :]
    ).astype(jnp.float32)
    flipped = flip_flags.astype(jnp.float32)
    plain_coef = jnp.einsum(
        "pk,pkg->pg", weights * (1.0 - flipped), onehot, precision=lax.Precision.HIGHEST
    )
    turned_coef = jnp.einsum(
        "pk,pkg->pg", weights * flipped, onehot, precision=lax.Precision.HIGHEST
    )
    coupling = jnp.dot(plain_coef, neighbours, precision=lax.Precision.HIGHEST)
    blocks = neighbours.reshape(group_size, V, V)
    turned = jnp.einsum("pg,gca->pac", turned_coef, blocks, precision=lax.Precision.HIGHEST)
    coupling = coupling + turned.reshape(pair_count, V * V)
    return ladder + coupling


def solution(mesh):
    placed = (
        P(("aux", "pair"), None),
        P("aux", None),
        P(("aux", "pair"), None),
        P(("aux", "pair"), None),
        P(("aux", "pair"), None),
    )
    return jax.shard_map(
        local, mesh=mesh, in_specs=placed, out_specs=P(("aux", "pair"), None), check_vma=False
    )
```

profile of v0, /device:TPU:6, one launch (start us, length us, event | category | flops | bytes accessed | tf_op | source)
XLA Modules:
  0.0 396.9 jit_solution(9041273356372757135)
XLA Ops:
  6.5 0.7 all-gather.6.cloned.1.call-update
  7.3 0.7 all-gather.4.cloned.1.call-update
  8.0 1.8 squeeze.9
  9.8 0.7 and_select_fusion
  10.5 0.7 subtract_multiply_fusion
  11.4 0.2 fusion.34
  11.6 37.3 %all-gather.6.cloned.1.call-done = bf16[16,2,36864]{2,1,0:T(2,128)(2,1)} async-done(((bf16[1,2,36864]{2,1,0:T(2,128)(2,1)}), bf16[16,2,36864]{2,1,0:T(2,128)(2,1)}) %all-gather.6.cloned.1.call-update) | async-done | bytes 2359312 | tf_op jit(solution)/shard_map/all_gather | solution.py:44
  48.9 6.0 %reshape.13 = bf16[32,192,192]{2,1,0:T(8,128)(2,1)S(1)} reshape(bf16[16,2,36864]{2,1,0:T(2,128)(2,1)} %all-gather.6.cloned.1.call-done) | data formatting | bytes 4718592 | tf_op jit(solution)/shard_map/reshape | solution.py:58
  54.9 2.6 fusion.30
  57.7 0.3 reshape.14
  58.0 2.9 reshape.16
  61.0 214.3 %all-gather.4.cloned.1.call-done = bf16[256,36864]{1,0:T(8,128)(2,1)} async-done(((bf16[16,36864]{1,0:T(8,128)(2,1)}), bf16[256,36864]{1,0:T(8,128)(2,1)}) %all-gather.4.cloned.1.call-update) | async-done | bytes 18874384 | tf_op jit(solution)/shard_map/all_gather | solution.py:43
  275.3 38.6 %reshape_reshape.4 = bf16[16,16,192,192]{3,2,1,0:T(8,128)(2,1)} reshape(bf16[256,36864]{1,0:T(8,128)(2,1)} %all-gather.4.cloned.1.call-done) | data formatting | bytes 37748736 | tf_op jit(solution)/shard_map/reshape;reshape | solution.py:17
  313.9 74.1 %while.18 = (s32[]{:T(128)}, f32[2,192,192]{2,1,0:T(8,128)S(1)}, bf16[16,16,192,192]{3,2,1,0:T(8,128)(2,1)}, bf16[2,192,192]{2,1,0:T(8,128)(2,1)S(1)}, s32[]{:T(128)}, /*index=5*/s32[]{:T(128)}) while((s32[]{:T(128)}, f32[2,192,192]{2,1,0:T(8,128)S(1)}, bf16[16,16,192,192]{3,2,1,0:T(8,128)(2,1)}, ...), condition=%wide.region_1.2_spmd.clone, body=%wide.region_0.1_spmd.clone.sunk | while | flops 907296768 | bytes 3884630 | solution.py:35
  313.9 4.6 %fusion.52 = f32[2,192,192]{2,1,0:T(8,128)S(1)} fusion(bf16[16,16,192,192]{3,2,1,0:T(8,128)(2,1)} %get-tuple-element.104, s32[]{:T(128)S(6)} %copy.23, f32[2,192,192]{2,1,0:T(8,128)S(1)} %get-tuple-element.97, bf16[2,192,192]{2,1,0:T(8,128)(2,1)S(1)} %get-tuple-element.105, pred[]{:T(512)S(6)} %compare.4), kind=kOutput, calls=%fused_computation.7.clone.1 | convolution fusion | flops 907296768 | bytes 3884544 | tf_op jit(solution)/shard_map/while/body/eval_jaxpr/while/body/eval_jaxpr/pqac,qdc->pad/dot_general | solution.py:28
  318.5 4.6 %fusion.52 = f32[2,192,192]{2,1,0:T(8,128)S(1)} fusion(bf16[16,16,192,192]{3,2,1,0:T(8,128)(2,1)} %get-tuple-element.104, s32[]{:T(128)S(6)} %copy.23, f32[2,192,192]{2,1,0:T(8,128)S(1)} %get-tuple-element.97, bf16[2,192,192]{2,1,0:T(8,128)(2,1)S(1)} %get-tuple-element.105, pred[]{:T(512)S(6)} %compare.4), kind=kOutput, calls=%fused_computation.7.clone.1 | convolution fusion | flops 907296768 | bytes 3884544 | tf_op jit(solution)/shard_map/while/body/eval_jaxpr/while/body/eval_jaxpr/pqac,qdc->pad/dot_general | solution.py:28
  323.1 4.6 %fusion.52 = f32[2,192,192]{2,1,0:T(8,128)S(1)} fusion(bf16[16,16,192,192]{3,2,1,0:T(8,128)(2,1)} %get-tuple-element.104, s32[]{:T(128)S(6)} %copy.23, f32[2,192,192]{2,1,0:T(8,128)S(1)} %get-tuple-element.97, bf16[2,192,192]{2,1,0:T(8,128)(2,1)S(1)} %get-tuple-element.105, pred[]{:T(512)S(6)} %compare.4), kind=kOutput, calls=%fused_computation.7.clone.1 | convolution fusion | flops 907296768 | bytes 3884544 | tf_op jit(solution)/shard_map/while/body/eval_jaxpr/while/body/eval_jaxpr/pqac,qdc->pad/dot_general | solution.py:28
  327.7 4.6 %fusion.52 = f32[2,192,192]{2,1,0:T(8,128)S(1)} fusion(bf16[16,16,192,192]{3,2,1,0:T(8,128)(2,1)} %get-tuple-element.104, s32[]{:T(128)S(6)} %copy.23, f32[2,192,192]{2,1,0:T(8,128)S(1)} %get-tuple-element.97, bf16[2,192,192]{2,1,0:T(8,128)(2,1)S(1)} %get-tuple-element.105, pred[]{:T(512)S(6)} %compare.4), kind=kOutput, calls=%fused_computation.7.clone.1 | convolution fusion | flops 907296768 | bytes 3884544 | tf_op jit(solution)/shard_map/while/body/eval_jaxpr/while/body/eval_jaxpr/pqac,qdc->pad/dot_general | solution.py:28
  332.3 4.6 %fusion.52 = f32[2,192,192]{2,1,0:T(8,128)S(1)} fusion(bf16[16,16,192,192]{3,2,1,0:T(8,128)(2,1)} %get-tuple-element.104, s32[]{:T(128)S(6)} %copy.23, f32[2,192,192]{2,1,0:T(8,128)S(1)} %get-tuple-element.97, bf16[2,192,192]{2,1,0:T(8,128)(2,1)S(1)} %get-tuple-element.105, pred[]{:T(512)S(6)} %compare.4), kind=kOutput, calls=%fused_computation.7.clone.1 | convolution fusion | flops 907296768 | bytes 3884544 | tf_op jit(solution)/shard_map/while/body/eval_jaxpr/while/body/eval_jaxpr/pqac,qdc->pad/dot_general | solution.py:28
  336.9 4.7 %fusion.52 = f32[2,192,192]{2,1,0:T(8,128)S(1)} fusion(bf16[16,16,192,192]{3,2,1,0:T(8,128)(2,1)} %get-tuple-element.104, s32[]{:T(128)S(6)} %copy.23, f32[2,192,192]{2,1,0:T(8,128)S(1)} %get-tuple-element.97, bf16[2,192,192]{2,1,0:T(8,128)(2,1)S(1)} %get-tuple-element.105, pred[]{:T(512)S(6)} %compare.4), kind=kOutput, calls=%fused_computation.7.clone.1 | convolution fusion | flops 907296768 | bytes 3884544 | tf_op jit(solution)/shard_map/while/body/eval_jaxpr/while/body/eval_jaxpr/pqac,qdc->pad/dot_general | solution.py:28
  341.6 4.6 %fusion.52 = f32[2,192,192]{2,1,0:T(8,128)S(1)} fusion(bf16[16,16,192,192]{3,2,1,0:T(8,128)(2,1)} %get-tuple-element.104, s32[]{:T(128)S(6)} %copy.23, f32[2,192,192]{2,1,0:T(8,128)S(1)} %get-tuple-element.97, bf16[2,192,192]{2,1,0:T(8,128)(2,1)S(1)} %get-tuple-element.105, pred[]{:T(512)S(6)} %compare.4), kind=kOutput, calls=%fused_computation.7.clone.1 | convolution fusion | flops 907296768 | bytes 3884544 | tf_op jit(solution)/shard_map/while/body/eval_jaxpr/while/body/eval_jaxpr/pqac,qdc->pad/dot_general | solution.py:28
  346.3 4.7 %fusion.52 = f32[2,192,192]{2,1,0:T(8,128)S(1)} fusion(bf16[16,16,192,192]{3,2,1,0:T(8,128)(2,1)} %get-tuple-element.104, s32[]{:T(128)S(6)} %copy.23, f32[2,192,192]{2,1,0:T(8,128)S(1)} %get-tuple-element.97, bf16[2,192,192]{2,1,0:T(8,128)(2,1)S(1)} %get-tuple-element.105, pred[]{:T(512)S(6)} %compare.4), kind=kOutput, calls=%fused_computation.7.clone.1 | convolution fusion | flops 907296768 | bytes 3884544 | tf_op jit(solution)/shard_map/while/body/eval_jaxpr/while/body/eval_jaxpr/pqac,qdc->pad/dot_general | solution.py:28
  351.0 4.6 %fusion.52 = f32[2,192,192]{2,1,0:T(8,128)S(1)} fusion(bf16[16,16,192,192]{3,2,1,0:T(8,128)(2,1)} %get-tuple-element.104, s32[]{:T(128)S(6)} %copy.23, f32[2,192,192]{2,1,0:T(8,128)S(1)} %get-tuple-element.97, bf16[2,192,192]{2,1,0:T(8,128)(2,1)S(1)} %get-tuple-element.105, pred[]{:T(512)S(6)} %compare.4), kind=kOutput, calls=%fused_computation.7.clone.1 | convolution fusion | flops 907296768 | bytes 3884544 | tf_op jit(solution)/shard_map/while/body/eval_jaxpr/while/body/eval_jaxpr/pqac,qdc->pad/dot_general | solution.py:28
  355.7 4.6 %fusion.52 = f32[2,192,192]{2,1,0:T(8,128)S(1)} fusion(bf16[16,16,192,192]{3,2,1,0:T(8,128)(2,1)} %get-tuple-element.104, s32[]{:T(128)S(6)} %copy.23, f32[2,192,192]{2,1,0:T(8,128)S(1)} %get-tuple-element.97, bf16[2,192,192]{2,1,0:T(8,128)(2,1)S(1)} %get-tuple-element.105, pred[]{:T(512)S(6)} %compare.4), kind=kOutput, calls=%fused_computation.7.clone.1 | convolution fusion | flops 907296768 | bytes 3884544 | tf_op jit(solution)/shard_map/while/body/eval_jaxpr/while/body/eval_jaxpr/pqac,qdc->pad/dot_general | solution.py:28
  360.3 4.6 %fusion.52 = f32[2,192,192]{2,1,0:T(8,128)S(1)} fusion(bf16[16,16,192,192]{3,2,1,0:T(8,128)(2,1)} %get-tuple-element.104, s32[]{:T(128)S(6)} %copy.23, f32[2,192,192]{2,1,0:T(8,128)S(1)} %get-tuple-element.97, bf16[2,192,192]{2,1,0:T(8,128)(2,1)S(1)} %get-tuple-element.105, pred[]{:T(512)S(6)} %compare.4), kind=kOutput, calls=%fused_computation.7.clone.1 | convolution fusion | flops 907296768 | bytes 3884544 | tf_op jit(solution)/shard_map/while/body/eval_jaxpr/while/body/eval_jaxpr/pqac,qdc->pad/dot_general | solution.py:28
  364.9 4.6 %fusion.52 = f32[2,192,192]{2,1,0:T(8,128)S(1)} fusion(bf16[16,16,192,192]{3,2,1,0:T(8,128)(2,1)} %get-tuple-element.104, s32[]{:T(128)S(6)} %copy.23, f32[2,192,192]{2,1,0:T(8,128)S(1)} %get-tuple-element.97, bf16[2,192,192]{2,1,0:T(8,128)(2,1)S(1)} %get-tuple-element.105, pred[]{:T(512)S(6)} %compare.4), kind=kOutput, calls=%fused_computation.7.clone.1 | convolution fusion | flops 907296768 | bytes 3884544 | tf_op jit(solution)/shard_map/while/body/eval_jaxpr/while/body/eval_jaxpr/pqac,qdc->pad/dot_general | solution.py:28
  369.5 4.6 %fusion.52 = f32[2,192,192]{2,1,0:T(8,128)S(1)} fusion(bf16[16,16,192,192]{3,2,1,0:T(8,128)(2,1)} %get-tuple-element.104, s32[]{:T(128)S(6)} %copy.23, f32[2,192,192]{2,1,0:T(8,128)S(1)} %get-tuple-element.97, bf16[2,192,192]{2,1,0:T(8,128)(2,1)S(1)} %get-tuple-element.105, pred[]{:T(512)S(6)} %compare.4), kind=kOutput, calls=%fused_computation.7.clone.1 | convolution fusion | flops 907296768 | bytes 3884544 | tf_op jit(solution)/shard_map/while/body/eval_jaxpr/while/body/eval_jaxpr/pqac,qdc->pad/dot_general | solution.py:28
  374.1 4.6 %fusion.52 = f32[2,192,192]{2,1,0:T(8,128)S(1)} fusion(bf16[16,16,192,192]{3,2,1,0:T(8,128)(2,1)} %get-tuple-element.104, s32[]{:T(128)S(6)} %copy.23, f32[2,192,192]{2,1,0:T(8,128)S(1)} %get-tuple-element.97, bf16[2,192,192]{2,1,0:T(8,128)(2,1)S(1)} %get-tuple-element.105, pred[]{:T(512)S(6)} %compare.4), kind=kOutput, calls=%fused_computation.7.clone.1 | convolution fusion | flops 907296768 | bytes 3884544 | tf_op jit(solution)/shard_map/while/body/eval_jaxpr/while/body/eval_jaxpr/pqac,qdc->pad/dot_general | solution.py:28
  378.7 4.7 %fusion.52 = f32[2,192,192]{2,1,0:T(8,128)S(1)} fusion(bf16[16,16,192,192]{3,2,1,0:T(8,128)(2,1)} %get-tuple-element.104, s32[]{:T(128)S(6)} %copy.23, f32[2,192,192]{2,1,0:T(8,128)S(1)} %get-tuple-element.97, bf16[2,192,192]{2,1,0:T(8,128)(2,1)S(1)} %get-tuple-element.105, pred[]{:T(512)S(6)} %compare.4), kind=kOutput, calls=%fused_computation.7.clone.1 | convolution fusion | flops 907296768 | bytes 3884544 | tf_op jit(solution)/shard_map/while/body/eval_jaxpr/while/body/eval_jaxpr/pqac,qdc->pad/dot_general | solution.py:28
  383.4 4.6 %fusion.52 = f32[2,192,192]{2,1,0:T(8,128)S(1)} fusion(bf16[16,16,192,192]{3,2,1,0:T(8,128)(2,1)} %get-tuple-element.104, s32[]{:T(128)S(6)} %copy.23, f32[2,192,192]{2,1,0:T(8,128)S(1)} %get-tuple-element.97, bf16[2,192,192]{2,1,0:T(8,128)(2,1)S(1)} %get-tuple-element.105, pred[]{:T(512)S(6)} %compare.4), kind=kOutput, calls=%fused_computation.7.clone.1 | convolution fusion | flops 907296768 | bytes 3884544 | tf_op jit(solution)/shard_map/while/body/eval_jaxpr/while/body/eval_jaxpr/pqac,qdc->pad/dot_general | solution.py:28
  388.0 0.3 reshape.12
  388.3 1.8 fusion.27
  (9 shorter events, 0.4 us)
Async XLA Ops:
  6.5 42.3 %all-gather.6.cloned.1.call-start = ((), (), s32[]{:S(2)}) async-start(), calls=%async_computation.1 | async-start | bytes 2506752 | tf_op jit(solution)/shard_map/all_gather | solution.py:44
  7.3 268.1 %all-gather.4.cloned.1.call-start = ((), (), s32[]{:S(2)}) async-start(), calls=%async_computation | async-start | bytes 20054016 | tf_op jit(solution)/shard_map/all_gather | solution.py:43
  60.9 252.9 %copy-start = (f32[2,192,192]{2,1,0:T(8,128)S(1)}, f32[2,192,192]{2,1,0:T(8,128)}, u32[]{:S(2)}) copy-start(f32[2,192,192]{2,1,0:T(8,128)} %custom-call) | copy-start | bytes 884740
  61.0 252.9 %copy-start.1 = (bf16[2,192,192]{2,1,0:T(8,128)(2,1)S(1)}, bf16[2,192,192]{2,1,0:T(8,128)(2,1)}, u32[]{:S(2)}) copy-start(bf16[2,192,192]{2,1,0:T(8,128)(2,1)} %squeeze.9) | copy-start | bytes 442372
Sparse Core Ops, SparseCore 0:
  9.2 39.6 all-gather.5
  51.4 223.9 all-gather.3
where the time goes:
time: 398 us; the launch traced here: 397 us
  waiting for transfers between devices  253 us (64%)
  matrix products  78.5 us (20%)
  local copies, waits for them, and re-layouts  50.1 us (13%)
  between operations  13.5 us (3%)
    all_gather x1, waiting for transfers between devices, local(): lax.all_gather(factors, 'aux', axis=0, tiled=True)  214 us
    dot_general x16, matrix products, advance(): jnp.einsum('pqac,qdc->pad', halfway, factor_set, preferred_element_type=j...  73.7 us
    another operation x1, local copies, waits for them, and re-layouts, ladder_terms(): fac_blocks.reshape(aux_count // aux_step, aux_step, virtual, virtual)  38.6 us
    all_gather x1, waiting for transfers between devices, local(): lax.all_gather(amplitudes, 'pair', axis=0, tiled=True).astype(jnp.float32)  37.3 us
  transfers between devices with their start and end apart: 2, of which 2 were waited for; matrix products, arithmetic and copies ran while one was open for 4% of the time, Pallas kernels for 0%

commit v1 on v0

--- a/solution.py
+++ b/solution.py
@@ -40,7 +40,12 @@
 
 def local(amplitudes, factors, sources, weights, flip_flags):
     pair_count = amplitudes.shape[0]
-    ladder = ladder_terms(amplitudes, lax.all_gather(factors, "aux", axis=0, tiled=True))
+    ladder = ladder_terms(
+        amplitudes,
+        jnp.concatenate(
+            lax.all_to_all(jnp.stack([factors] * lax.axis_size("aux")), "aux", 0, 0), axis=0
+        ),
+    )
     neighbours = lax.all_gather(amplitudes, "pair", axis=0, tiled=True).astype(jnp.float32)
     group_size = neighbours.shape[0]
     local_index = sources % group_size

time: 398 us -> 591 us (1.48)
  the two profiles are of different devices: /device:TPU:6 before, /device:TPU:174 now
where the time goes in v1:
time: 591 us; the launch traced here: 590 us
  waiting for transfers between devices  431 us (73%)
  matrix products  78.5 us (13%)
  local copies, waits for them, and re-layouts  56.8 us (10%)
  between operations  13.5 us (2%)
  starting transfers between devices  9.78 us (2%)
    all_to_all x1, waiting for transfers between devices, local(): lax.all_to_all(jnp.stack([factors] * lax.axis_size('aux')), 'aux', 0, 0)  285 us
    all_gather x1, waiting for transfers between devices, local(): lax.all_gather(amplitudes, 'pair', axis=0, tiled=True).astype(jnp.float32)  145 us
    dot_general x16, matrix products, advance(): jnp.einsum('pqac,qdc->pad', halfway, factor_set, preferred_element_type=j...  73.7 us
    another operation x1, local copies, waits for them, and re-layouts, ladder_terms(): fac_blocks.reshape(aux_count // aux_step, aux_step, virtual, virtual)  38.6 us
  transfers between devices with their start and end apart: 2, of which 2 were waited for; matrix products, arithmetic and copies ran while one was open for 2% of the time, Pallas kernels for 0%

profile of v1, /device:TPU:174, one launch (start us, length us, event | category | flops | bytes accessed | tf_op | source)
XLA Modules:
  0.0 589.7 jit_solution(15852117560583145320)
XLA Ops:
  6.5 7.6 %stack.2 = bf16[16,16,36864]{2,1,0:T(8,128)(2,1)} broadcast(bf16[16,36864]{1,0:T(8,128)(2,1)} %param.8), dimensions={1,2} | broadcast | bytes 20054016 | tf_op jit(solution)/shard_map/stack | solution.py:46
  14.1 9.7 %all-to-all-start = ((bf16[16,16,36864]{2,1,0:T(8,128)(2,1)}), bf16[16,16,36864]{2,1,0:T(8,128)(2,1)}, u32[]{:S(2)}, u32[]{:S(2)}) async-start(bf16[16,16,36864]{2,1,0:T(8,128)(2,1)} %stack.2), calls=%async_computation | async-start | bytes 37748736 | tf_op jit(solution)/shard_map/all_to_all | solution.py:46
  23.9 0.7 all-gather.3.cloned.1.call-update
  24.6 0.9 squeeze.9
  25.8 0.2 fusion.34
  26.0 145.3 %all-gather.3.cloned.1.call-done = bf16[16,2,36864]{2,1,0:T(2,128)(2,1)} async-done(((bf16[1,2,36864]{2,1,0:T(2,128)(2,1)}), bf16[16,2,36864]{2,1,0:T(2,128)(2,1)}) %all-gather.3.cloned.1.call-update) | async-done | bytes 2359312 | tf_op jit(solution)/shard_map/all_gather | solution.py:49
  171.3 6.0 %reshape.15 = bf16[32,192,192]{2,1,0:T(8,128)(2,1)S(1)} reshape(bf16[16,2,36864]{2,1,0:T(2,128)(2,1)} %all-gather.3.cloned.1.call-done) | data formatting | bytes 4718592 | tf_op jit(solution)/shard_map/reshape | solution.py:63
  177.3 2.6 fusion.30
  179.9 0.2 copy.10
  180.1 0.3 reshape.16
  180.4 2.9 reshape.18
  183.4 284.8 %all-to-all-done = bf16[16,16,36864]{2,1,0:T(8,128)(2,1)} async-done(((bf16[16,16,36864]{2,1,0:T(8,128)(2,1)}), bf16[16,16,36864]{2,1,0:T(8,128)(2,1)}, u32[]{:S(2)}, u32[]{:S(2)}) %all-to-all-start) | async-done | bytes 18874400 | tf_op jit(solution)/shard_map/all_to_all | solution.py:46
  468.2 38.6 %reshape_reshape_reshape.3 = bf16[16,16,192,192]{3,2,1,0:T(8,128)(2,1)} reshape(bf16[16,16,36864]{2,1,0:T(8,128)(2,1)} %all-to-all-done) | data formatting | bytes 37748736 | tf_op jit(solution)/shard_map/reshape;reshape;reshape | solution.py:17
  506.8 74.0 %while.18 = (s32[]{:T(128)}, f32[2,192,192]{2,1,0:T(8,128)S(1)}, bf16[16,16,192,192]{3,2,1,0:T(8,128)(2,1)}, bf16[2,192,192]{2,1,0:T(8,128)(2,1)S(1)}, s32[]{:T(128)}, /*index=5*/s32[]{:T(128)}) while((s32[]{:T(128)}, f32[2,192,192]{2,1,0:T(8,128)S(1)}, bf16[16,16,192,192]{3,2,1,0:T(8,128)(2,1)}, ...), condition=%wide.region_1.2_spmd.clone, body=%wide.region_0.1_spmd.clone.sunk | while | flops 907296768 | bytes 3884630 | solution.py:35
  506.8 4.6 fusion.52
  511.4 4.6 fusion.52
  516.0 4.6 fusion.52
  520.6 4.6 fusion.52
  525.2 4.7 fusion.52
  529.8 4.6 fusion.52
  534.5 4.6 fusion.52
  539.2 4.6 fusion.52
  543.8 4.6 fusion.52
  548.5 4.6 fusion.52
  553.1 4.6 fusion.52
  557.7 4.6 fusion.52
  562.3 4.6 fusion.52
  567.0 4.6 fusion.52
  571.6 4.6 fusion.52
  576.2 4.6 fusion.52
  580.8 0.3 reshape.14
  581.1 1.8 fusion.27
  (17 shorter events, 0.3 us)
Async XLA Ops:
  14.1 10.5 %copy-start = (bf16[2,36864]{1,0:T(2,128)(2,1)S(1)}, bf16[2,36864]{1,0:T(2,128)(2,1)}, u32[]{:S(2)}) copy-start(bf16[2,36864]{1,0:T(2,128)(2,1)} %param.7) | copy-start | bytes 442372
  14.1 11.4 %copy-start.3 = (s32[2,8]{1,0:T(2,128)S(1)}, s32[2,8]{1,0:T(2,128)}, u32[]{:S(2)}) copy-start(s32[2,8]{1,0:T(2,128)} %param.9) | copy-start | bytes 196
  14.1 11.4 %copy-start.4 = (f32[2,8]{1,0:T(2,128)S(1)}, f32[2,8]{1,0:T(2,128)}, u32[]{:S(2)}) copy-start(f32[2,8]{1,0:T(2,128)} %param.10) | copy-start | bytes 196
  14.1 11.4 %copy-start.5 = (s32[2,8]{1,0:T(2,128)S(1)}, s32[2,8]{1,0:T(2,128)}, u32[]{:S(2)}) copy-start(s32[2,8]{1,0:T(2,128)} %param.11) | copy-start | bytes 196
  14.1 454.0 %all-to-all-start = ((bf16[16,16,36864]{2,1,0:T(8,128)(2,1)}), bf16[16,16,36864]{2,1,0:T(8,128)(2,1)}, u32[]{:S(2)}, u32[]{:S(2)}) async-start(bf16[16,16,36864]{2,1,0:T(8,128)(2,1)} %stack.2), calls=%async_computation | async-start | bytes 37748736 | tf_op jit(solution)/shard_map/all_to_all | solution.py:46
  23.9 147.4 %all-gather.3.cloned.1.call-start = ((), (), s32[]{:S(2)}) async-start(), calls=%async_computation.1 | async-start | bytes 2506752 | tf_op jit(solution)/shard_map/all_gather | solution.py:49
  183.3 323.4 %copy-start.1 = (f32[2,192,192]{2,1,0:T(8,128)S(1)}, f32[2,192,192]{2,1,0:T(8,128)}, u32[]{:S(2)}) copy-start(f32[2,192,192]{2,1,0:T(8,128)} %custom-call) | copy-start | bytes 884740
  183.4 323.4 %copy-start.2 = (bf16[2,192,192]{2,1,0:T(8,128)(2,1)S(1)}, bf16[2,192,192]{2,1,0:T(8,128)(2,1)}, u32[]{:S(2)}) copy-start(bf16[2,192,192]{2,1,0:T(8,128)(2,1)} %squeeze.9) | copy-start | bytes 442372
Sparse Core Ops, SparseCore 0:
  26.5 144.6 all-gather.2
